TPU v7x, 32 devices: a whole 2x2x4 slice. The times are simulated.
32 devices in a mesh: req: 8 (over z, x), grp: 4 (over y, core).
Axes of the slice: x: 2, y: 2, z: 4, core: 2. Of those that a mesh axis runs over, the one named last changes fastest.
Arguments:
- hidden: bfloat16 [256, 16, 1024], P(('grp', 'req')), parts along dimension 0, may hold values from -6 to 6
- norm_gain: float32 [1024], replicated, may hold values from 0.1 to 1.9
- in_weight: bfloat16 [1024, 4096], replicated, may hold values from -0.1875 to 0.1875
- conv_weight: float32 [4, 2048], P(None, 'req'), may hold values from -3 to 3
- conv_bias: float32 [2048], P('req'), may hold values from -3 to 3
- x_weight: bfloat16 [2048, 160], P('req'), may hold values from -0.125 to 0.125
- step_weight: bfloat16 [128, 2048], P(None, 'req'), may hold values from -0.5 to 0.5
- step_bias: float32 [2048], P('req'), may hold values from -5 to -1
- log_decay: float32 [16, 2048], P(None, 'req'), may hold values from -0.7 to 2.8
- skip_gain: float32 [2048], P('req'), may hold values from 0.5 to 1.5
- out_weight: bfloat16 [2048, 1024], replicated, may hold values from -0.125 to 0.125
- old_states: float32 [256, 16, 2048], P(('grp', 'req')), parts along dimension 0, may hold values from -3 to 3
- old_edges: bfloat16 [256, 3, 2048], P(('grp', 'req')), parts along dimension 0, may hold values from -6 to 6
- anchor: int32 [256], P('grp'), parts along dimension 0, may hold values from 0 to 63, each once
- fresh_flag: int32 [256], P('grp'), parts along dimension 0, may hold values 0 or 1
- accepted: int32 [256], P('grp'), parts along dimension 0, may hold values from 1 to 16
- request_ages: int32 [256], P('grp'), parts along dimension 0, may hold values from 0 to 7
Outputs:
- layer_out: bfloat16 [256, 16, 1024], P(('grp', 'req')), parts along dimension 0
- new_states: float32 [256, 16, 2048], P(('grp', 'req')), parts along dimension 0
There are 4 independent parts, one for each index of `grp`. A program takes and returns all parts, laid end to end along the dimension named above; an argument that names none is the same for every part. Nothing has to cross between parts.
Inputs may be any that keep to these rules, and one draw needn't show every extreme that they name: Every old slot is the anchor of exactly one request.
All inputs are finite; a program needn't handle non-finite values.
Results may differ from a plain program's by a relative error of at most 0.0091.
Values may be sent and summed in bfloat16 or wider, within the bound.
No kernel may reach another device: no remote copies, remote signals or barrier semaphores. Data moves between devices by JAX's collectives and lax.ppermute only.
A program may use at most 128 MiB of HBM per device.

v0:
```python
import jax
import jax.numpy as jnp
from jax import lax
from jax.sharding import PartitionSpec as P

EPS = 1e-05


def rms_normed(values_in, norm_gain):
    values = values_in.astype(jnp.float32)
    factor = lax.rsqrt(jnp.mean(values * values, axis=-1, keepdims=True) + EPS)
    return (values * factor * norm_gain).astype(jnp.bfloat16)


def on_device(
    hidden,
    norm_gain,
    in_weight,
    conv_weight,
    conv_bias,
    x_weight,
    step_weight,
    step_bias,
    log_decay,
    skip_gain,
    out_weight,
    old_states,
    old_edges,
    anchor,
    fresh_flag,
    accepted,
    request_ages,
):
    local_reqs, draft_len, width = hidden.shape
    inner_width = out_weight.shape[0]
    channels = conv_weight.shape[1]
    state_size = log_decay.shape[0]
    low_rank = step_weight.shape[0]
    span = old_edges.shape[1]
    state_lead = jnp.swapaxes(old_states, 0, 1)
    edge_lead = jnp.swapaxes(old_edges.astype(jnp.float32), 0, 1)
    moved_states, moved_edges = (
        lax.all_to_all(state_lead, "req", split_axis=2, concat_axis=1, tiled=True),
        lax.all_to_all(edge_lead, "req", split_axis=2, concat_axis=1, tiled=True),
    )
    token_major = jnp.swapaxes(hidden, 0, 1).reshape(draft_len * local_reqs, width)
    normed = rms_normed(token_major, norm_gain)
    projected = jnp.dot(normed, in_weight, preferred_element_type=jnp.float32).astype(jnp.bfloat16)
    projected = jnp.moveaxis(projected.reshape(draft_len, local_reqs, 2, inner_width), 2, 0)
    grouped = lax.all_to_all(projected, "req", split_axis=3, concat_axis=2, tiled=True)
    all_reqs = grouped.shape[2]
    inner_part = grouped[0]
    gate_part = grouped[1]
    keep_state = (1 - fresh_flag).astype(jnp.float32)
    start_state = jnp.take(moved_states, anchor, axis=1) * keep_state[None, :, None]
    edges = jnp.take(moved_edges, anchor, axis=1)
    distance = span - jnp.arange(span, dtype=jnp.int32)
    usable = (distance[:, None] <= request_ages[None, :]) & (fresh_flag[None, :] == 0)
    history = jnp.where(usable[:, :, None], edges, jnp.zeros((), jnp.float32))
    sequence = jnp.concatenate([history, inner_part.astype(jnp.float32)], axis=0)
    running = conv_bias + conv_weight[0] * sequence[0:draft_len]
    for offset in range(1, conv_weight.shape[0]):
        running = running + conv_weight[offset] * sequence[offset : offset + draft_len]
    conv_out = jax.nn.silu(running).astype(jnp.bfloat16)
    conv_rows = conv_out.reshape(draft_len * all_reqs, channels)
    partial_value = jnp.dot(conv_rows, x_weight, preferred_element_type=jnp.float32)
    mixed_rows = lax.psum(partial_value, "req").astype(jnp.bfloat16)
    flat = all_reqs * channels
    step_sizes = jax.nn.softplus(
        jnp.dot(mixed_rows[:, :low_rank], step_weight, preferred_element_type=jnp.float32)
        + step_bias
    )
    step_sizes = step_sizes.reshape(draft_len, flat)
    coeffs = (
        mixed_rows[:, low_rank:].astype(jnp.float32).reshape(draft_len, all_reqs, 2 * state_size)
    )
    b_coeff = coeffs[:, :, :state_size]
    c_coeff = coeffs[:, :, state_size:]
    inputs = conv_out.astype(jnp.float32)
    flat_inputs = inputs.reshape(draft_len, flat)
    decay = jnp.broadcast_to(
        (-jnp.exp(log_decay))[:, None, :], (state_size, all_reqs, channels)
    ).reshape(state_size, flat)
    start_flat = start_state.reshape(state_size, flat)

    def spread(per_token):
        return jnp.broadcast_to(
            jnp.swapaxes(per_token, 0, 1)[:, :, None], (state_size, all_reqs, channels)
        ).reshape(state_size, flat)

    def advance(carried, sliced):
        current, chosen = carried
        step_delta, step_b, step_c, step_input, step_index = sliced
        factor = jnp.exp(step_delta[None, :] * decay)
        current = factor * current + (step_delta * step_input)[None, :] * spread(step_b)
        result = jnp.sum(spread(step_c) * current, axis=0)
        picked = jnp.broadcast_to(
            (accepted == step_index + 1)[:, None], (all_reqs, channels)
        ).reshape(flat)
        chosen = jnp.where(picked[None, :], current, chosen)
        return ((current, chosen), result)

    sliced = (step_sizes, b_coeff, c_coeff, flat_inputs, jnp.arange(draft_len, dtype=jnp.int32))
    (final_state, chosen), outputs = lax.scan(advance, (start_flat, start_flat), sliced)
    outputs = outputs.reshape(draft_len, all_reqs, channels)
    gated_rows = (
        (outputs + skip_gain * inputs) * jax.nn.silu(gate_part.astype(jnp.float32))
    ).astype(jnp.bfloat16)
    returned = lax.all_to_all(gated_rows, "req", split_axis=1, concat_axis=2, tiled=True)
    layer_out = jnp.dot(
        returned.reshape(draft_len * local_reqs, inner_width),
        out_weight,
        preferred_element_type=jnp.float32,
    ).astype(jnp.bfloat16)
    layer_out = jnp.swapaxes(layer_out.reshape(draft_len, local_reqs, width), 0, 1)
    owned = lax.all_to_all(
        chosen.reshape(state_size, all_reqs, channels),
        "req",
        split_axis=1,
        concat_axis=2,
        tiled=True,
    )
    return (layer_out, jnp.swapaxes(owned, 0, 1))


def solution(mesh):
    return jax.shard_map(
        on_device,
        mesh=mesh,
        in_specs=(
            P(("grp", "req"), None, None),
            P(),
            P(),
            P(None, "req"),
            P("req"),
            P("req", None),
            P(None, "req"),
            P("req"),
            P(None, "req"),
            P("req"),
            P(),
            P(("grp", "req"), None, None),
            P(("grp", "req"), None, None),
            P("grp"),
            P("grp"),
            P("grp"),
            P("grp"),
        ),
        out_specs=(P(("grp", "req"), None, None), P(("grp", "req"), None, None)),
        check_vma=False,
    )
```

profile of v0, /device:TPU:0, one launch (start us, length us, event | category | flops | bytes accessed | tf_op | source)
XLA Modules:
  0.0 369.8 jit_solution(14479661632174473123)
XLA Ops:
  0.7 4.0 %copy.100 = f32[8,3,2048]{0,1,2:T(4,128)} copy(bf16[8,3,2048]{2,0,1:T(8,128)(2,1)} %param.31) | data formatting | bytes 294912 | tf_op jit(solution)/shard_map/transpose | solution.py:41
  4.7 3.9 %bitcast_bitcast_fusion.2 = f32[2048,3,8]{2,1,0:T(4,128)} fusion(f32[8,3,2048]{0,1,2:T(4,128)} %copy.100), kind=kLoop, calls=%fused_computation.72 | loop fusion | bytes 393216
  8.6 5.1 %reshape.188 = f32[8,1,6144]{2,1,0:T(1,128)} reshape(f32[2048,3,8]{2,1,0:T(4,128)} %bitcast_bitcast_fusion.2) | data formatting | bytes 393216
  13.7 7.3 %all-to-all-start.1 = ((f32[8,1,6144]{2,1,0:T(1,128)}), f32[8,1,6144]{2,1,0:T(1,128)S(1)}, u32[]{:S(2)}, u32[]{:S(2)}) async-start(f32[8,1,6144]{2,1,0:T(1,128)} %reshape.188), calls=%async_computation.1 | async-start | bytes 393216 | tf_op jit(solution)/shard_map/all_to_all | solution.py:44
  20.9 4.7 %copy.94 = f32[8,16,2048]{1,0,2:T(8,128)} copy(f32[8,16,2048]{2,1,0:T(8,128)S(1)} %copy-done.3) | data formatting | bytes 2097152 | tf_op args[11]
  26.0 4.8 %convolution_convert_fusion = bf16[128,4096]{1,0:T(8,128)(2,1)S(1)} fusion(bf16[1024,4096]{1,0:T(8,128)(2,1)} %param.21, f32[1024]{0:T(1024)S(1)} %copy-done.4, f32[128]{0:T(128)S(1)} %rsqrt.12, bf16[8,16,1024]{2,1,0:T(8,128)(2,1)S(1)} %copy-done.2), kind=kOutput, calls=%fused_computation.11 | convolution fusion | flops 1074790400 | bytes 9703936 | tf_op jit(solution)/shard_map/dot_general | solution.py:48
  30.8 8.9 %copy.103 = bf16[16,8,2,2048]{0,1,2,3:T(8,128)(2,1)} copy(bf16[16,8,2,2048]{3,1,2,0:T(8,128)(2,1)S(1)} %bitcast.169) | data formatting | bytes 2097152 | tf_op jit(solution)/shard_map/reshape | solution.py:49
  39.6 7.5 %bitcast_bitcast_fusion = bf16[2048,2,8,16]{3,2,1,0:T(8,128)(2,1)} fusion(bf16[16,8,2,2048]{0,1,2,3:T(8,128)(2,1)} %copy.103), kind=kLoop, calls=%fused_computation.70 | loop fusion | bytes 2097152
  47.1 5.8 %bitcast_bitcast_fusion.1 = f32[2048,8,16]{2,1,0:T(8,128)} fusion(f32[8,16,2048]{1,0,2:T(8,128)} %copy.94), kind=kLoop, calls=%fused_computation.71 | loop fusion | bytes 2097152
  52.9 8.1 %reshape.184 = f32[8,1,32768]{2,1,0:T(1,128)} reshape(f32[2048,8,16]{2,1,0:T(8,128)} %bitcast_bitcast_fusion.1) | data formatting | bytes 2097152
  61.1 6.0 %all-to-all-start = ((f32[8,1,32768]{2,1,0:T(1,128)}), f32[8,1,32768]{2,1,0:T(1,128)S(1)}, u32[]{:S(2)}, u32[]{:S(2)}) async-start(f32[8,1,32768]{2,1,0:T(1,128)} %reshape.184), calls=%async_computation | async-start | bytes 2097152 | tf_op jit(solution)/shard_map/all_to_all | solution.py:43
  67.3 11.3 %reshape.186 = bf16[8,2,32768]{2,1,0:T(2,128)(2,1)} reshape(bf16[2048,2,8,16]{3,2,1,0:T(8,128)(2,1)} %bitcast_bitcast_fusion) | data formatting | bytes 2097152
  80.5 4.7 %reshape.189 = f32[2048,3,8]{2,1,0:T(4,128)} reshape(f32[8,6144]{1,0:T(8,128)S(1)} %reduce.3) | data formatting | bytes 393216
  92.5 3.7 %all-to-all-start.2 = ((bf16[8,2,32768]{2,1,0:T(2,128)(2,1)}), bf16[8,2,32768]{2,1,0:T(2,128)(2,1)S(1)}, u32[]{:S(2)}, u32[]{:S(2)}) async-start(bf16[8,2,32768]{2,1,0:T(2,128)(2,1)} %reshape.186), calls=%async_computation.2 | async-start | bytes 2097152 | tf_op jit(solution)/shard_map/all_to_all | solution.py:50
  99.4 6.1 %reshape.185 = f32[2048,8,16]{2,1,0:T(8,128)} reshape(f32[8,32768]{1,0:T(8,128)S(1)} %reduce.2) | data formatting | bytes 2097152
  105.5 5.4 %copy.96 = f32[16,8,8,256]{3,2,1,0:T(8,128)S(1)} copy(f32[16,8,8,256]{0,2,3,1:T(8,128)} %bitcast.155) | data formatting | bytes 2097152 | tf_op jit(solution)/shard_map/all_to_all | solution.py:43
  112.4 9.5 %all-to-all-done.2 = bf16[8,2,32768]{2,1,0:T(2,128)(2,1)S(1)} async-done(((bf16[8,2,32768]{2,1,0:T(2,128)(2,1)}), bf16[8,2,32768]{2,1,0:T(2,128)(2,1)S(1)}, u32[]{:S(2)}, u32[]{:S(2)}) %all-to-all-start.2) | async-done | bytes 1048608 | tf_op jit(solution)/shard_map/all_to_all | solution.py:50
  121.9 7.6 %reshape.187 = bf16[2048,2,8,16]{3,2,1,0:T(8,128)(2,1)} reshape(bf16[8,2,32768]{2,1,0:T(2,128)(2,1)S(1)} %all-to-all-done.2) | data formatting | bytes 2097152
  129.5 8.9 %copy.104 = bf16[2,16,8,8,256]{4,2,3,1,0:T(8,128)(2,1)S(1)} copy(bf16[2,16,8,8,256]{1,2,0,4,3:T(8,128)(2,1)} %bitcast.156) | data formatting | bytes 2097152 | tf_op jit(solution)/shard_map/all_to_all | solution.py:50
  140.2 43.6 %all-reduce.1 = bf16[1024,160]{0,1:T(8,128)(2,1)} all-reduce(f32[1024,160]{0,1:T(8,128)S(1)} %fusion.29), channel_id=1, replica_groups=mesh['req'=8,'grp'=4] {'req'}, use_global_device_ids=true, to_apply=%region_1.2 | all-reduce | flops 163840 | bytes 983040 | tf_op jit(solution)/shard_map/psum | solution.py:67
  191.2 132.7 %while.15 = (s32[]{:T(128)}, f32[16,16384]{1,0:T(8,128)S(1)}, f32[16,16384]{1,0:T(8,128)S(1)}, f32[16,16384]{1,0:T(8,128)}, f32[16,16384]{1,0:T(8,128)}, /*index...) while((s32[]{:T(128)}, f32[16,16384]{1,0:T(8,128)S(1)}, ...), condition=%wide.region_4.5_spmd.clone, body=%wide.region_2.4_spmd.clone.sunk | while | flops 1835075 | bytes 18522676 | solution.py:104
  332.7 9.4 %all-to-all-done.3 = bf16[16,64,256]{2,0,1:T(8,128)(2,1)S(1)} async-done(((bf16[16,64,256]{2,0,1:T(8,128)(2,1)}), bf16[16,64,256]{2,0,1:T(8,128)(2,1)S(1)}, u32[]{:S(2)}, u32[]{:S(2)}) %all-to-all-start.3) | async-done | bytes 524320 | tf_op jit(solution)/shard_map/all_to_all | solution.py:109
  342.1 9.1 %all-to-all-start.4 = ((f32[16,64,256]{2,0,1:T(8,128)}), f32[16,64,256]{2,0,1:T(8,128)S(1)}, u32[]{:S(2)}, u32[]{:S(2)}) async-start(f32[16,64,256]{2,0,1:T(8,128)} %bitcast.121), calls=%async_computation.4 | async-start | bytes 2097152 | tf_op jit(solution)/shard_map/all_to_all | solution.py:116
  355.4 12.2 %all-to-all-done.4 = f32[16,64,256]{2,0,1:T(8,128)S(1)} async-done(((f32[16,64,256]{2,0,1:T(8,128)}), f32[16,64,256]{2,0,1:T(8,128)S(1)}, u32[]{:S(2)}, u32[]{:S(2)}) %all-to-all-start.4) | async-done | bytes 1048608 | tf_op jit(solution)/shard_map/all_to_all | solution.py:116
  (323 shorter events, 159.0 us)
Async XLA Ops:
  0.6 139.3 %copy-start = (bf16[256,160]{0,1:T(8,128)(2,1)S(1)}, bf16[256,160]{0,1:T(8,128)(2,1)}, u32[]{:S(2)}) copy-start(bf16[256,160]{0,1:T(8,128)(2,1)} %param.24) | copy-start | bytes 245764
  0.6 20.3 %copy-start.3 = (f32[8,16,2048]{2,1,0:T(8,128)S(1)}, f32[8,16,2048]{2,1,0:T(8,128)}, u32[]{:S(2)}) copy-start(f32[8,16,2048]{2,1,0:T(8,128)} %param.30) | copy-start | bytes 3145732
  8.6 17.1 %copy-start.2 = (bf16[8,16,1024]{2,1,0:T(8,128)(2,1)S(1)}, bf16[8,16,1024]{2,1,0:T(8,128)(2,1)}, u32[]{:S(2)}) copy-start(bf16[8,16,1024]{2,1,0:T(8,128)(2,1)} %param.19) | copy-start | bytes 786436
  8.6 17.4 %copy-start.4 = (f32[1024]{0:T(1024)S(1)}, f32[1024]{0:T(1024)}, u32[]{:S(2)}) copy-start(f32[1024]{0:T(1024)} %param.20) | copy-start | bytes 12292
  13.7 47.4 %all-to-all-start.1 = ((f32[8,1,6144]{2,1,0:T(1,128)}), f32[8,1,6144]{2,1,0:T(1,128)S(1)}, u32[]{:S(2)}, u32[]{:S(2)}) async-start(f32[8,1,6144]{2,1,0:T(1,128)} %reshape.188), calls=%async_computation.1 | async-start | bytes 393216 | tf_op jit(solution)/shard_map/all_to_all | solution.py:44
  52.9 8.2 %copy-start.12 = (s32[64]{0:T(128)S(1)}, s32[64]{0:T(128)}, u32[]{:S(2)}) copy-start(s32[64]{0:T(128)} %param.33) | copy-start | bytes 772
  52.9 14.3 %copy-start.13 = (s32[64]{0:T(128)S(1)}, s32[64]{0:T(128)}, u32[]{:S(2)}) copy-start(s32[64]{0:T(128)} %param.32) | copy-start | bytes 772
  52.9 25.7 %copy-start.9 = (s32[64]{0:T(128)S(1)}, s32[64]{0:T(128)}, u32[]{:S(2)}) copy-start(s32[64]{0:T(128)} %param.35) | copy-start | bytes 772
  52.9 25.9 %copy-start.6 = (f32[4,256]{1,0:T(4,128)S(1)}, f32[4,256]{1,0:T(4,128)}, u32[]{:S(2)}) copy-start(f32[4,256]{1,0:T(4,128)} %param.22) | copy-start | bytes 12292
  52.9 25.9 %copy-start.5 = (f32[16,256]{1,0:T(8,128)S(1)}, f32[16,256]{1,0:T(8,128)}, u32[]{:S(2)}) copy-start(f32[16,256]{1,0:T(8,128)} %param.27) | copy-start | bytes 49156
  61.1 31.4 %all-to-all-start = ((f32[8,1,32768]{2,1,0:T(1,128)}), f32[8,1,32768]{2,1,0:T(1,128)S(1)}, u32[]{:S(2)}, u32[]{:S(2)}) async-start(f32[8,1,32768]{2,1,0:T(1,128)} %reshape.184), calls=%async_computation | async-start | bytes 2097152 | tf_op jit(solution)/shard_map/all_to_all | solution.py:43
  92.5 29.4 %all-to-all-start.2 = ((bf16[8,2,32768]{2,1,0:T(2,128)(2,1)}), bf16[8,2,32768]{2,1,0:T(2,128)(2,1)S(1)}, u32[]{:S(2)}, u32[]{:S(2)}) async-start(bf16[8,2,32768]{2,1,0:T(2,128)(2,1)} %reshape.186), calls=%async_computation.2 | async-start | bytes 2097152 | tf_op jit(solution)/shard_map/all_to_all | solution.py:50
  112.4 27.0 %copy-start.7 = (f32[256]{0:T(256)S(1)}, f32[256]{0:T(256)}, u32[]{:S(2)}) copy-start(f32[256]{0:T(256)} %param.23) | copy-start | bytes 3076
  129.5 55.2 %copy-start.10 = (bf16[128,256]{1,0:T(8,128)(2,1)S(1)}, bf16[128,256]{1,0:T(8,128)(2,1)}, u32[]{:S(2)}) copy-start(bf16[128,256]{1,0:T(8,128)(2,1)} %param.25) | copy-start | bytes 196612
  129.5 55.2 %copy-start.11 = (f32[256]{0:T(256)S(1)}, f32[256]{0:T(256)}, u32[]{:S(2)}) copy-start(f32[256]{0:T(256)} %param.26) | copy-start | bytes 3076
  138.4 1.0 copy-start.1
  138.4 52.8 %copy-start.14 = (s32[64]{0:T(128)S(1)}, s32[64]{0:T(128)}, u32[]{:S(2)}) copy-start(s32[64]{0:T(128)} %param.34) | copy-start | bytes 772
  191.2 134.3 %copy-start.8 = (f32[256]{0:T(256)S(1)}, f32[256]{0:T(256)}, u32[]{:S(2)}) copy-start(f32[256]{0:T(256)} %param.28) | copy-start | bytes 3076
  328.1 14.0 %all-to-all-start.3 = ((bf16[16,64,256]{2,0,1:T(8,128)(2,1)}), bf16[16,64,256]{2,0,1:T(8,128)(2,1)S(1)}, u32[]{:S(2)}, u32[]{:S(2)}) async-start(bf16[16,64,256]{2,0,1:T(8,128)(2,1)} %copy.108), calls=%async_computation.3 | async-start | bytes 1048576 | tf_op jit(solution)/shard_map/all_to_all | solution.py:109
  342.1 25.5 %all-to-all-start.4 = ((f32[16,64,256]{2,0,1:T(8,128)}), f32[16,64,256]{2,0,1:T(8,128)S(1)}, u32[]{:S(2)}, u32[]{:S(2)}) async-start(f32[16,64,256]{2,0,1:T(8,128)} %bitcast.121), calls=%async_computation.4 | async-start | bytes 2097152 | tf_op jit(solution)/shard_map/all_to_all | solution.py:116
where the time goes:
time: 372 us; the launch traced here: 370 us
  local copies, waits for them, and re-layouts  191 us (51%)
  other arithmetic  47.8 us (13%)
  blocking collectives  43.6 us (12%)
  waiting for transfers between devices  33.9 us (9%)
  starting transfers between devices  29.5 us (8%)
  loops' own time  12.3 us (3%)
  matrix products  10.8 us (3%)
    unnamed x47, local copies, waits for them, and re-layouts  70.4 us
    psum x1, blocking collectives, on_device(): mixed_rows = lax.psum(partial_value, 'req').astype(jnp.bfloat16)  43.6 us
    dynamic_update_slice x16, local copies, waits for them, and re-layouts, on_device(): lax.scan(advance, (start_flat, start_flat), sliced)  31.1 us
    while x48, local copies, waits for them, and re-layouts  29.4 us
    dynamic_slice x16, other arithmetic, on_device(): lax.scan(advance, (start_flat, start_flat), sliced)  20.9 us
    reduce_sum x16, other arithmetic, advance(): result = jnp.sum(spread(step_c) * current, axis=0)  14.9 us
    another operation x1, loops' own time, on_device(): lax.scan(advance, (start_flat, start_flat), sliced)  12.3 us
    all_to_all x1, waiting for transfers between devices, on_device(): lax.all_to_all(chosen.reshape(state_size, all_reqs, channels), 'req', spl...  12.2 us
  transfers between devices with their start and end apart: 5, of which 4 were waited for; matrix products, arithmetic and copies ran while one was open for 23% of the time, Pallas kernels for 0%

commit v1 on v0

--- a/solution.py
+++ b/solution.py
@@ -64,7 +64,7 @@
     conv_out = jax.nn.silu(running).astype(jnp.bfloat16)
     conv_rows = conv_out.reshape(draft_len * all_reqs, channels)
     partial_value = jnp.dot(conv_rows, x_weight, preferred_element_type=jnp.float32)
-    mixed_rows = lax.psum(partial_value, "req").astype(jnp.bfloat16)
+    mixed_rows = jnp.sum(lax.all_gather(partial_value, "req"), axis=0).astype(jnp.bfloat16)
     flat = all_reqs * channels
     step_sizes = jax.nn.softplus(
         jnp.dot(mixed_rows[:, :low_rank], step_weight, preferred_element_type=jnp.float32)

time: 372 us -> 429 us (1.15)
  waiting for transfers between devices: 33.9 us -> 105 us
  blocking collectives: 43.6 us -> 0 us
  local copies, waits for them, and re-layouts: 191 us -> 212 us
  between operations: 1.01 us -> 14.4 us
  starting transfers between devices: 29.5 us -> 24.4 us
    psum x1 -> x0, blocking collectives: 43.6 us -> none  [on_device(): mixed_rows = lax.psum(partial_value, 'req').astype(jnp.bfloat16)]
    all_to_all x1, waiting for transfers between devices: 2.88 us -> 44.4 us  [on_device(): lax.all_to_all(state_lead, 'req', split_axis=2, concat_axis=1, tiled=True)]
    dynamic_slice x32, local copies, waits for them, and re-layouts: 10.9 us -> 23.1 us  [on_device(): lax.scan(advance, (start_flat, start_flat), sliced)]
    all_gather x0 -> x1, waiting for transfers between devices: none -> 10.9 us  [on_device(): lax.all_gather(partial_value, 'req')]
    all_to_all x1, waiting for transfers between devices: 12.2 us -> 21.7 us  [on_device(): lax.all_to_all(chosen.reshape(state_size, all_reqs, channels), 'req', spl...]
    unnamed x47 -> x48, local copies, waits for them, and re-layouts: 70.4 us -> 78.3 us
    all_to_all x1, starting transfers between devices: 9.06 us -> 3.62 us  [on_device(): lax.all_to_all(chosen.reshape(state_size, all_reqs, channels), 'req', spl...]
    all_to_all x1, waiting for transfers between devices: 9.5 us -> 14.2 us  [on_device(): lax.all_to_all(projected, 'req', split_axis=3, concat_axis=2, tiled=True)]
  transfers between devices with their start and end apart: 5 -> 6, of which waited for: 4 -> 5; matrix products, arithmetic and copies ran while one was open for 23% -> 21% of each run, Pallas kernels for 0% -> 0%
where the time goes in v1:
time: 429 us; the launch traced here: 426 us
  local copies, waits for them, and re-layouts  212 us (49%)
  waiting for transfers between devices  105 us (24%)
  other arithmetic  48.4 us (11%)
  starting transfers between devices  24.4 us (6%)
  between operations  14.4 us (3%)
  loops' own time  11.6 us (3%)
  matrix products  10.6 us (2%)
    unnamed x48, local copies, waits for them, and re-layouts  78.3 us
    all_to_all x1, waiting for transfers between devices, on_device(): lax.all_to_all(state_lead, 'req', split_axis=2, concat_axis=1, tiled=True)  44.4 us
    dynamic_update_slice x16, local copies, waits for them, and re-layouts, on_device(): lax.scan(advance, (start_flat, start_flat), sliced)  31 us
    while x48, local copies, waits for them, and re-layouts  29.4 us
    dynamic_slice x32, local copies, waits for them, and re-layouts, on_device(): lax.scan(advance, (start_flat, start_flat), sliced)  23.1 us
    all_to_all x1, waiting for transfers between devices, on_device(): lax.all_to_all(chosen.reshape(state_size, all_reqs, channels), 'req', spl...  21.7 us
    dynamic_slice x16, other arithmetic, on_device(): lax.scan(advance, (start_flat, start_flat), sliced)  20.9 us
    reduce_sum x16, other arithmetic, advance(): result = jnp.sum(spread(step_c) * current, axis=0)  14.9 us
  transfers between devices with their start and end apart: 6, of which 5 were waited for; matrix products, arithmetic and copies ran while one was open for 21% of the time, Pallas kernels for 0%

profile of v1, /device:TPU:0, one launch (start us, length us, event | category | flops | bytes accessed | tf_op | source)
XLA Modules:
  0.0 425.9 jit_solution(15233959858914909926)
XLA Ops:
  7.2 3.9 copy.98
  11.1 3.9 bitcast_bitcast_fusion.2
  15.1 5.1 %reshape.189 = f32[8,1,6144]{2,1,0:T(1,128)} reshape(f32[2048,3,8]{2,1,0:T(4,128)} %bitcast_bitcast_fusion.2) | data formatting | bytes 393216
  20.1 7.3 %all-to-all-start.1 = ((f32[8,1,6144]{2,1,0:T(1,128)}), f32[8,1,6144]{2,1,0:T(1,128)S(1)}, u32[]{:S(2)}, u32[]{:S(2)}) async-start(f32[8,1,6144]{2,1,0:T(1,128)} %reshape.189), calls=%async_computation.1 | async-start | bytes 393216 | tf_op jit(solution)/shard_map/all_to_all | solution.py:44
  27.7 4.8 %convolution_convert_fusion = bf16[128,4096]{1,0:T(8,128)(2,1)S(1)} fusion(bf16[1024,4096]{1,0:T(8,128)(2,1)} %param.21, f32[1024]{0:T(1024)S(1)} %copy-done.4, f32[128]{0:T(128)S(1)} %rsqrt.12, bf16[8,16,1024]{2,1,0:T(8,128)(2,1)S(1)} %copy-done.3), kind=kOutput, calls=%fused_computation.12 | convolution fusion | flops 1074790400 | bytes 9703936 | tf_op jit(solution)/shard_map/dot_general | solution.py:48
  32.5 8.8 %copy.101 = bf16[16,8,2,2048]{0,1,2,3:T(8,128)(2,1)} copy(bf16[16,8,2,2048]{3,1,2,0:T(8,128)(2,1)S(1)} %bitcast.175) | data formatting | bytes 2097152 | tf_op jit(solution)/shard_map/reshape | solution.py:49
  41.3 7.5 %bitcast_bitcast_fusion = bf16[2048,2,8,16]{3,2,1,0:T(8,128)(2,1)} fusion(bf16[16,8,2,2048]{0,1,2,3:T(8,128)(2,1)} %copy.101), kind=kLoop, calls=%fused_computation.71 | loop fusion | bytes 2097152
  48.8 11.3 %reshape.187 = bf16[8,2,32768]{2,1,0:T(2,128)(2,1)} reshape(bf16[2048,2,8,16]{3,2,1,0:T(8,128)(2,1)} %bitcast_bitcast_fusion) | data formatting | bytes 2097152
  60.1 6.0 %all-to-all-start.2 = ((bf16[8,2,32768]{2,1,0:T(2,128)(2,1)}), bf16[8,2,32768]{2,1,0:T(2,128)(2,1)S(1)}, u32[]{:S(2)}, u32[]{:S(2)}) async-start(bf16[8,2,32768]{2,1,0:T(2,128)(2,1)} %reshape.187), calls=%async_computation.2 | async-start | bytes 2097152 | tf_op jit(solution)/shard_map/all_to_all | solution.py:50
  68.3 4.7 %reshape.190 = f32[2048,3,8]{2,1,0:T(4,128)} reshape(f32[8,6144]{1,0:T(8,128)S(1)} %reduce.3) | data formatting | bytes 393216
  77.4 14.2 %all-to-all-done.2 = bf16[8,2,32768]{2,1,0:T(2,128)(2,1)S(1)} async-done(((bf16[8,2,32768]{2,1,0:T(2,128)(2,1)}), bf16[8,2,32768]{2,1,0:T(2,128)(2,1)S(1)}, u32[]{:S(2)}, u32[]{:S(2)}) %all-to-all-start.2) | async-done | bytes 1048608 | tf_op jit(solution)/shard_map/all_to_all | solution.py:50
  91.5 7.5 %reshape.188 = bf16[2048,2,8,16]{3,2,1,0:T(8,128)(2,1)} reshape(bf16[8,2,32768]{2,1,0:T(2,128)(2,1)S(1)} %all-to-all-done.2) | data formatting | bytes 2097152
  99.1 8.9 %copy.102 = bf16[2,16,8,8,256]{4,2,3,1,0:T(8,128)(2,1)S(1)} copy(bf16[2,16,8,8,256]{1,2,0,4,3:T(8,128)(2,1)} %bitcast.160) | data formatting | bytes 2097152 | tf_op jit(solution)/shard_map/all_to_all | solution.py:50
  109.8 6.0 %copy.92 = f32[8,16,2048]{1,0,2:T(8,128)} copy(f32[8,16,2048]{2,1,0:T(8,128)} %param.30) | data formatting | bytes 2097152 | tf_op args[11]
  115.8 6.6 %bitcast_bitcast_fusion.1 = f32[2048,8,16]{2,1,0:T(8,128)} fusion(f32[8,16,2048]{1,0,2:T(8,128)} %copy.92), kind=kLoop, calls=%fused_computation.72 | loop fusion | bytes 2097152
  122.3 8.1 %reshape.185 = f32[8,1,32768]{2,1,0:T(1,128)} reshape(f32[2048,8,16]{2,1,0:T(8,128)} %bitcast_bitcast_fusion.1) | data formatting | bytes 2097152
  135.8 44.4 %all-to-all-done = f32[8,1,32768]{2,1,0:T(1,128)S(1)} async-done(((f32[8,1,32768]{2,1,0:T(1,128)}), f32[8,1,32768]{2,1,0:T(1,128)S(1)}, u32[]{:S(2)}, u32[]{:S(2)}) %all-to-all-start) | async-done | bytes 1048608 | tf_op jit(solution)/shard_map/all_to_all | solution.py:43
  183.4 6.0 %reshape.186 = f32[2048,8,16]{2,1,0:T(8,128)} reshape(f32[8,32768]{1,0:T(8,128)S(1)} %reduce.2) | data formatting | bytes 2097152
  189.4 5.6 %copy.94 = f32[16,8,8,256]{3,2,1,0:T(8,128)S(1)} copy(f32[16,8,8,256]{0,2,3,1:T(8,128)} %bitcast.161) | data formatting | bytes 2097152 | tf_op jit(solution)/shard_map/all_to_all | solution.py:43
  196.6 10.9 %all-gather.3.cloned.1.call-done = f32[8192,160]{0,1:T(8,128)} async-done(((f32[1024,160]{0,1:T(8,128)}), f32[8192,160]{0,1:T(8,128)}) %all-gather.3.cloned.1.call-update) | async-done | bytes 5242896 | tf_op jit(solution)/shard_map/all_gather | solution.py:67
  207.5 6.8 %copy.122 = f32[20,8,8,1024]{3,2,1,0:T(8,128)S(1)} copy(f32[20,8,8,1024]{3,1,2,0:T(8,128)} %bitcast.168) | data formatting | bytes 10485760
  220.6 144.1 %while.15 = (s32[]{:T(128)}, f32[16,16384]{1,0:T(8,128)S(1)}, f32[16,16384]{1,0:T(8,128)S(1)}, f32[16,16384]{1,0:T(8,128)}, f32[16,16384]{1,0:T(8,128)}, /*index...) while((s32[]{:T(128)}, f32[16,16384]{1,0:T(8,128)S(1)}, ...), condition=%wide.region_4.5_spmd.clone, body=%wide.region_2.4_spmd.clone.sunk | while | flops 1835075 | bytes 18522668 | solution.py:104
  373.5 13.8 %all-to-all-done.3 = bf16[16,64,256]{2,0,1:T(8,128)(2,1)S(1)} async-done(((bf16[16,64,256]{2,0,1:T(8,128)(2,1)}), bf16[16,64,256]{2,0,1:T(8,128)(2,1)S(1)}, u32[]{:S(2)}, u32[]{:S(2)}) %all-to-all-start.3) | async-done | bytes 524320 | tf_op jit(solution)/shard_map/all_to_all | solution.py:109
  395.1 21.7 %all-to-all-done.4 = f32[16,64,256]{2,0,1:T(8,128)S(1)} async-done(((f32[16,64,256]{2,0,1:T(8,128)}), f32[16,64,256]{2,0,1:T(8,128)S(1)}, u32[]{:S(2)}, u32[]{:S(2)}) %all-to-all-start.4) | async-done | bytes 1048608 | tf_op jit(solution)/shard_map/all_to_all | solution.py:116
  (327 shorter events, 176.1 us)
Async XLA Ops:
  7.2 101.4 %copy-start = (bf16[256,160]{0,1:T(8,128)(2,1)S(1)}, bf16[256,160]{0,1:T(8,128)(2,1)}, u32[]{:S(2)}) copy-start(bf16[256,160]{0,1:T(8,128)(2,1)} %param.24) | copy-start | bytes 245764
  11.1 16.3 %copy-start.3 = (bf16[8,16,1024]{2,1,0:T(8,128)(2,1)S(1)}, bf16[8,16,1024]{2,1,0:T(8,128)(2,1)}, u32[]{:S(2)}) copy-start(bf16[8,16,1024]{2,1,0:T(8,128)(2,1)} %param.19) | copy-start | bytes 786436
  11.1 16.6 %copy-start.4 = (f32[1024]{0:T(1024)S(1)}, f32[1024]{0:T(1024)}, u32[]{:S(2)}) copy-start(f32[1024]{0:T(1024)} %param.20) | copy-start | bytes 12292
  20.1 40.0 %all-to-all-start.1 = ((f32[8,1,6144]{2,1,0:T(1,128)}), f32[8,1,6144]{2,1,0:T(1,128)S(1)}, u32[]{:S(2)}, u32[]{:S(2)}) async-start(f32[8,1,6144]{2,1,0:T(1,128)} %reshape.189), calls=%async_computation.1 | async-start | bytes 393216 | tf_op jit(solution)/shard_map/all_to_all | solution.py:44
  48.8 17.5 %copy-start.13 = (s32[64]{0:T(128)S(1)}, s32[64]{0:T(128)}, u32[]{:S(2)}) copy-start(s32[64]{0:T(128)} %param.33) | copy-start | bytes 772
  48.8 17.6 %copy-start.9 = (s32[64]{0:T(128)S(1)}, s32[64]{0:T(128)}, u32[]{:S(2)}) copy-start(s32[64]{0:T(128)} %param.35) | copy-start | bytes 772
  48.8 17.8 %copy-start.12 = (s32[64]{0:T(128)S(1)}, s32[64]{0:T(128)}, u32[]{:S(2)}) copy-start(s32[64]{0:T(128)} %param.32) | copy-start | bytes 772
  48.8 17.8 %copy-start.6 = (f32[4,256]{1,0:T(4,128)S(1)}, f32[4,256]{1,0:T(4,128)}, u32[]{:S(2)}) copy-start(f32[4,256]{1,0:T(4,128)} %param.22) | copy-start | bytes 12292
  60.1 31.4 %all-to-all-start.2 = ((bf16[8,2,32768]{2,1,0:T(2,128)(2,1)}), bf16[8,2,32768]{2,1,0:T(2,128)(2,1)S(1)}, u32[]{:S(2)}, u32[]{:S(2)}) async-start(bf16[8,2,32768]{2,1,0:T(2,128)(2,1)} %reshape.187), calls=%async_computation.2 | async-start | bytes 2097152 | tf_op jit(solution)/shard_map/all_to_all | solution.py:50
  66.1 141.4 %all-gather.3.cloned.1.call-start = ((), (), s32[]{:S(2)}) async-start(), calls=%async_computation.5 | async-start | bytes 5898240 | tf_op jit(solution)/shard_map/all_gather | solution.py:67
  99.1 9.0 %copy-start.7 = (f32[256]{0:T(256)S(1)}, f32[256]{0:T(256)}, u32[]{:S(2)}) copy-start(f32[256]{0:T(256)} %param.23) | copy-start | bytes 3076
  108.0 7.8 %copy-start.2 = (bf16[2,16,8,8,256]{4,2,3,1,0:T(8,128)(2,1)}, bf16[2,16,8,8,256]{4,2,3,1,0:T(8,128)(2,1)S(1)}, u32[]{:S(2)}) copy-start(bf16[2,16,8,8,256]{4,2,3,1,0:T(8,128)(2,1)S(1)} %copy.102) | copy-start | bytes 3145732
  122.3 12.1 %copy-start.5 = (f32[16,256]{1,0:T(8,128)S(1)}, f32[16,256]{1,0:T(8,128)}, u32[]{:S(2)}) copy-start(f32[16,256]{1,0:T(8,128)} %param.27) | copy-start | bytes 49156
  130.5 49.8 %all-to-all-start = ((f32[8,1,32768]{2,1,0:T(1,128)}), f32[8,1,32768]{2,1,0:T(1,128)S(1)}, u32[]{:S(2)}, u32[]{:S(2)}) async-start(f32[8,1,32768]{2,1,0:T(1,128)} %reshape.185), calls=%async_computation | async-start | bytes 2097152 | tf_op jit(solution)/shard_map/all_to_all | solution.py:43
  214.3 2.2 copy-start.10
  214.3 2.2 copy-start.11
  214.3 6.3 %copy-start.14 = (s32[64]{0:T(128)S(1)}, s32[64]{0:T(128)}, u32[]{:S(2)}) copy-start(s32[64]{0:T(128)} %param.34) | copy-start | bytes 772
  220.6 145.6 %copy-start.8 = (f32[256]{0:T(256)S(1)}, f32[256]{0:T(256)}, u32[]{:S(2)}) copy-start(f32[256]{0:T(256)} %param.28) | copy-start | bytes 3076
  368.8 18.4 %all-to-all-start.3 = ((bf16[16,64,256]{2,0,1:T(8,128)(2,1)}), bf16[16,64,256]{2,0,1:T(8,128)(2,1)S(1)}, u32[]{:S(2)}, u32[]{:S(2)}) async-start(bf16[16,64,256]{2,0,1:T(8,128)(2,1)} %copy.106), calls=%async_computation.3 | async-start | bytes 1048576 | tf_op jit(solution)/shard_map/all_to_all | solution.py:109
  387.2 29.6 %all-to-all-start.4 = ((f32[16,64,256]{2,0,1:T(8,128)}), f32[16,64,256]{2,0,1:T(8,128)S(1)}, u32[]{:S(2)}, u32[]{:S(2)}) async-start(f32[16,64,256]{2,0,1:T(8,128)} %bitcast.126), calls=%async_computation.4 | async-start | bytes 2097152 | tf_op jit(solution)/shard_map/all_to_all | solution.py:116
  391.2 27.9 %copy-start.1 = (bf16[256,160]{0,1:T(8,128)(2,1)S(1)}, bf16[256,160]{0,1:T(8,128)(2,1)}, u32[]{:S(2)}) copy-start(bf16[256,160]{0,1:T(8,128)(2,1)} %param.24) | copy-start | bytes 245764
Sparse Core Ops, SparseCore 0:
  109.9 97.5 all-gather.2
